TPU v7x, 256 devices: a whole 4x4x8 slice. The times are simulated.
256 devices in a mesh: blk: 64 (over x, y_hi, z), con: 4 (over y_lo, core).
Axes of the slice: x: 4, y: 4 (y_hi: 2, y_lo: 2; y = y_hi * 2 + y_lo), z: 8, core: 2. Of those that a mesh axis runs over, the one named last changes fastest.
Arguments:
- patch_rows: bfloat16 [4, 12288, 16, 1024], P('con', 'blk'), may hold values from -6 to 6
- subject_ids: int32 [12288], replicated, may hold values from 0 to 3071
- logit_scale: float32 [2], replicated, may hold values from 5 to 20
- logit_bias: float32 [2], replicated, may hold values from -6 to -2
Outputs:
- grad_emb: float32 [4, 12288, 1024], P('con', 'blk')
All inputs are finite; a program needn't handle non-finite values.
Results may differ from a plain program's by a relative error of at most 0.0037.
Values may be sent and summed in bfloat16 or wider, within the bound.
No kernel may reach another device: no remote copies, remote signals or barrier semaphores. Data moves between devices by JAX's collectives and lax.ppermute only.
A program may use at most 128 MiB of HBM per device.

v0:
```python
import jax
import jax.numpy as jnp
from jax import lax
from jax.sharding import PartitionSpec as P


def from_partner(shard, axis, stride):
    return lax.ppermute(shard, axis, [(i, i ^ 1 << stride) for i in range(lax.axis_size(axis))])


def on_device(patch_rows, subject_ids, logit_scale, logit_bias):
    row_count = patch_rows.shape[1]
    patch_count = patch_rows.shape[2]
    width = patch_rows.shape[3]
    pooled = jnp.sum(patch_rows[0], axis=1, dtype=jnp.float32) / patch_count
    row_norms = jnp.sqrt(jnp.sum(pooled * pooled, axis=1, keepdims=True) + 1e-06)
    own_emb = (pooled / row_norms).astype(jnp.bfloat16)
    contrast = lax.axis_index("con")
    pair_index = contrast // 2
    scale_value = logit_scale[pair_index]
    bias_value = logit_bias[pair_index]
    position = lax.axis_index("blk")
    own_ids = lax.dynamic_slice_in_dim(subject_ids, position * row_count, row_count, 0)
    partner = from_partner(own_emb, "con", 0)
    shard_rows = lax.all_gather(partner, "blk", axis=0, tiled=True)
    logits = (
        scale_value
        * lax.dot_general(
            own_emb, shard_rows, (((1,), (1,)), ((), ())), preferred_element_type=jnp.float32
        )
        + bias_value
    )
    label_sign = jnp.where(own_ids[:, None] == subject_ids[None, :], 1.0, -1.0).astype(jnp.float32)
    coeff = (scale_value * (jax.nn.sigmoid(label_sign * logits) - 1.0) * label_sign).astype(
        jnp.bfloat16
    )
    gradient = jnp.dot(coeff, shard_rows, preferred_element_type=jnp.float32)
    return gradient.reshape(1, row_count, width)


def solution(mesh):
    in_specs = (P("con", "blk", None, None), P(), P(), P())
    out_specs = P("con", "blk", None)
    return jax.shard_map(
        on_device, mesh=mesh, in_specs=in_specs, out_specs=out_specs, check_vma=False
    )
```

profile of v0, /device:TPU:1, one launch (start us, length us, event | category | flops | bytes accessed | tf_op | source)
XLA Modules:
  0.0 312.9 jit_solution(6936567670982369488)
XLA Ops:
  6.5 0.0 copy-start.2
  6.5 0.0 copy-start.3
  6.5 0.0 copy-start.1
  6.5 0.0 all-gather.2.cloned.1.call-start
  6.5 6.1 %convert_reduce_fusion = f32[192,1024]{1,0:T(8,128)S(1)} fusion(bf16[1,192,16,1024]{3,2,1,0:T(8,128)(2,1)} %param.4), kind=kLoop, calls=%fused_computation.11 | loop fusion | flops 6094848 | bytes 7077888 | tf_op jit(solution)/shard_map/reduce_sum | solution.py:15
  12.6 0.2 multiply_reduce_fusion
  12.8 0.1 divide_convert_fusion
  12.9 3.3 %collective-permute-start = (bf16[192,1024]{1,0:T(8,128)(2,1)S(1)}, bf16[192,1024]{1,0:T(8,128)(2,1)S(1)}, u32[]{:S(2)}, u32[]{:S(2)}) collective-permute-start(bf16[192,1024]{1,0:T(8,128)(2,1)S(1)} %divide_convert_fusion), channel_id=1, source_target_pairs={{0,1},{1,0},{2,3},{3,2},{4,5},{5,4},{6,7},{7,6},{8,9},{9,8},{10,11... | collective-permute-start | bytes 1179656 | tf_op jit(solution)/shard_map/ppermute | solution.py:8
  16.2 1.3 collective-permute-done
  17.6 0.0 copy-start
  17.6 0.7 copy-done
  18.3 0.0 all-gather.2.cloned.1.call-update
  18.4 0.0 copy-done.2
  18.4 0.6 dynamic_slice.11
  19.0 0.0 copy-done.3
  19.0 0.6 dynamic_slice.9
  19.6 0.0 copy-done.1
  19.6 0.1 dynamic_slice.10
  19.7 258.4 %all-gather.2.cloned.1.call-done = bf16[12288,1024]{1,0:T(8,128)(2,1)} async-done(((bf16[192,1024]{1,0:T(8,128)(2,1)}), bf16[12288,1024]{1,0:T(8,128)(2,1)}) %all-gather.2.cloned.1.call-update) | async-done | bytes 25165840 | tf_op jit(solution)/shard_map/all_gather | solution.py:25
  278.2 27.9 %fusion.17 = f32[1,192,1024]{2,1,0:T(8,128)} fusion(bf16[12288,1024]{1,0:T(8,128)(2,1)} %all-gather.2.cloned.1.call-done, bf16[192,1024]{1,0:T(8,128)(2,1)S(1)} %divide_convert_fusion, f32[]{:T(128)} %bitcast.1, s32[12288]{0:T(1024)S(1)} %copy-done.1, f32[]{:T(128)} %bitcast, s32[192]{0:T(256)S(1)} %dynamic_slice.10), kind=kOutput, calls=%fused_computation.19 | convolution fusion | flops 9691987968 | bytes 26395400 | tf_op jit(solution)/shard_map/dot_general | solution.py:37
  (1 shorter events, 0.0 us)
Async XLA Ops:
  6.5 11.8 %copy-start.2 = (f32[2]{0:T(128)S(1)}, f32[2]{0:T(128)}, u32[]{:S(2)}) copy-start(f32[2]{0:T(128)} %param.7) | copy-start | bytes 28
  6.5 12.4 %copy-start.3 = (f32[2]{0:T(128)S(1)}, f32[2]{0:T(128)}, u32[]{:S(2)}) copy-start(f32[2]{0:T(128)} %param.6) | copy-start | bytes 28
  6.5 13.1 %copy-start.1 = (s32[12288]{0:T(1024)S(1)}, s32[12288]{0:T(1024)}, u32[]{:S(2)}) copy-start(s32[12288]{0:T(1024)} %param.5) | copy-start | bytes 147460
  6.5 271.6 %all-gather.2.cloned.1.call-start = ((), (), s32[]{:S(2)}) async-start(), calls=%async_computation | async-start | bytes 25559040 | tf_op jit(solution)/shard_map/all_gather | solution.py:25
  12.9 4.6 %collective-permute-start = (bf16[192,1024]{1,0:T(8,128)(2,1)S(1)}, bf16[192,1024]{1,0:T(8,128)(2,1)S(1)}, u32[]{:S(2)}, u32[]{:S(2)}) collective-permute-start(bf16[192,1024]{1,0:T(8,128)(2,1)S(1)} %divide_convert_fusion), channel_id=1, source_target_pairs={{0,1},{1,0},{2,3},{3,2},{4,5},{5,4},{6,7},{7,6},{8,9},{9,8},{10,11... | collective-permute-start | bytes 1179656 | tf_op jit(solution)/shard_map/ppermute | solution.py:8
  17.6 0.7 copy-start
Sparse Core Ops, SparseCore 0:
  18.5 259.6 all-gather.1
where the time goes:
time: 313 us
  waiting for transfers between devices  260 us (83%)
  matrix products  27.9 us (9%)
  between operations  13.4 us (4%)
  other arithmetic  6.38 us (2%)
  starting transfers between devices  3.29 us (1%)
    all_gather x1, waiting for transfers between devices, on_device(): shard_rows = lax.all_gather(partner, 'blk', axis=0, tiled=True)  258 us
    dot_general x1, matrix products, on_device(): gradient = jnp.dot(coeff, shard_rows, preferred_element_type=jnp.float32)  27.9 us
  transfers between devices with their start and end apart: 2, of which 2 were waited for; matrix products, arithmetic and copies ran while one was open for 0% of the time, Pallas kernels for 0%

commit v1 on v0

--- a/solution.py
+++ b/solution.py
@@ -22,7 +22,9 @@
     position = lax.axis_index("blk")
     own_ids = lax.dynamic_slice_in_dim(subject_ids, position * row_count, row_count, 0)
     partner = from_partner(own_emb, "con", 0)
-    shard_rows = lax.all_gather(partner, "blk", axis=0, tiled=True)
+    shard_rows = jnp.concatenate(
+        lax.all_to_all(jnp.stack([partner] * lax.axis_size("blk")), "blk", 0, 0), axis=0
+    )
     logits = (
         scale_value
         * lax.dot_general(

time: 313 us -> 680 us (2.17)
  the two profiles are of different devices: /device:TPU:1 before, /device:TPU:146 now
where the time goes in v1:
time: 680 us
  waiting for transfers between devices  622 us (91%)
  matrix products  28 us (4%)
  starting transfers between devices  13.1 us (2%)
  local copies, waits for them, and re-layouts  10 us (1%)
    all_to_all x1, waiting for transfers between devices, on_device(): lax.all_to_all(jnp.stack([partner] * lax.axis_size('blk')), 'blk', 0, 0)  620 us
    dot_general x1, matrix products, on_device(): gradient = jnp.dot(coeff, shard_rows, preferred_element_type=jnp.float32)  28 us
  transfers between devices with their start and end apart: 2, of which 2 were waited for; matrix products, arithmetic and copies ran while one was open for 0% of the time, Pallas kernels for 0%

profile of v1, /device:TPU:146, one launch (start us, length us, event | category | flops | bytes accessed | tf_op | source)
XLA Modules:
  0.0 679.6 jit_solution(5524196334629865819)
XLA Ops:
  0.0 6.1 convert_reduce_fusion
  6.1 0.2 multiply_reduce_fusion
  6.2 0.1 divide_convert_fusion
  6.4 0.1 collective-permute-start
  6.5 1.7 collective-permute-done
  8.2 8.6 %stack.2 = bf16[64,192,1024]{2,1,0:T(8,128)(2,1)} broadcast(bf16[192,1024]{1,0:T(8,128)(2,1)S(1)} %collective-permute-done), dimensions={1,2} | broadcast | bytes 25559040 | tf_op jit(solution)/shard_map/stack | solution.py:26
  16.8 0.0 copy-start.1
  16.9 0.0 copy-start.2
  16.9 0.0 copy-start
  16.9 13.0 %all-to-all-start = ((bf16[64,192,1024]{2,1,0:T(8,128)(2,1)}), bf16[64,192,1024]{2,1,0:T(8,128)(2,1)}, u32[]{:S(2)}, u32[]{:S(2)}) async-start(bf16[64,192,1024]{2,1,0:T(8,128)(2,1)} %stack.2), calls=%async_computation | async-start | bytes 50331648 | tf_op jit(solution)/shard_map/all_to_all | solution.py:26
  29.9 0.0 copy-done.1
  29.9 0.7 dynamic_slice.11
  30.5 0.0 copy-done.2
  30.5 0.6 dynamic_slice.9
  31.2 0.0 copy-done
  31.2 0.1 dynamic_slice.10
  31.2 620.4 %all-to-all-done = bf16[64,192,1024]{2,1,0:T(8,128)(2,1)} async-done(((bf16[64,192,1024]{2,1,0:T(8,128)(2,1)}), bf16[64,192,1024]{2,1,0:T(8,128)(2,1)}, u32[]{:S(2)}, u32[]{:S(2)}) %all-to-all-start) | async-done | bytes 25165856 | tf_op jit(solution)/shard_map/all_to_all | solution.py:26
  651.6 28.0 %fusion.17 = f32[1,192,1024]{2,1,0:T(8,128)} fusion(bf16[12288,1024]{1,0:T(8,128)(2,1)} %bitcast.1, bf16[192,1024]{1,0:T(8,128)(2,1)S(1)} %divide_convert_fusion, f32[]{:T(128)} %bitcast.2, s32[12288]{0:T(1024)S(1)} %copy-done, f32[]{:T(128)} %bitcast, s32[192]{0:T(256)S(1)} %dynamic_slice.10), kind=kOutput, calls=%fused_computation.19 | convolution fusion | flops 9691987968 | bytes 26395400 | tf_op jit(solution)/shard_map/dot_general | solution.py:39
  (1 shorter events, 0.0 us)
Async XLA Ops:
  6.4 1.8 collective-permute-start
  16.8 13.0 %copy-start.1 = (f32[2]{0:T(128)S(1)}, f32[2]{0:T(128)}, u32[]{:S(2)}) copy-start(f32[2]{0:T(128)} %param.7) | copy-start | bytes 28
  16.9 13.7 %copy-start.2 = (f32[2]{0:T(128)S(1)}, f32[2]{0:T(128)}, u32[]{:S(2)}) copy-start(f32[2]{0:T(128)} %param.6) | copy-start | bytes 28
  16.9 14.3 %copy-start = (s32[12288]{0:T(1024)S(1)}, s32[12288]{0:T(1024)}, u32[]{:S(2)}) copy-start(s32[12288]{0:T(1024)} %param.5) | copy-start | bytes 147460
  16.9 634.8 %all-to-all-start = ((bf16[64,192,1024]{2,1,0:T(8,128)(2,1)}), bf16[64,192,1024]{2,1,0:T(8,128)(2,1)}, u32[]{:S(2)}, u32[]{:S(2)}) async-start(bf16[64,192,1024]{2,1,0:T(8,128)(2,1)} %stack.2), calls=%async_computation | async-start | bytes 50331648 | tf_op jit(solution)/shard_map/all_to_all | solution.py:26
